TPU v7x, 256 devices: a whole 4x4x8 slice. The times are simulated.
256 devices in a mesh: grp: 8 (over y, core), mem: 32 (over x, z).
Axes of the slice: x: 4, y: 4, z: 8, core: 2. Of those that a mesh axis runs over, the one named last changes fastest.
Arguments:
- amplitudes: bfloat16 [8, 32, 384, 384], P('grp', 'mem'), may hold values from -6 to 6
- integrals: bfloat16 [8, 32, 384, 384], P('grp', 'mem'), may hold values from -0.3125 to 0.3125
- task_list: int32 [8, 2048, 3], P('grp'), may hold values from 0 to 31
- task_counts: int32 [8, 32], P('grp'), may hold values from 1 to 64, 1024 in all within a row
- owner_map: int32 [32], replicated, may hold values from 0 to 31, each once
Outputs:
- cycle: bfloat16 [8, 32, 384, 384], P('grp', 'mem')
Inputs may be any that keep to these rules, and one draw needn't show every extreme that they name: `task_list`: rows 64 * e to 64 * (e + 1) - 1 of a group are executor e's task slots; every id is a tile id. `task_counts`: the counts of a group sum to 1024. `owner_map`: A permutation of the tile ids.
All inputs are finite; a program needn't handle non-finite values.
Results may differ from a plain program's by a relative error of at most 0.014.
Values may be sent and summed in bfloat16 or wider, within the bound.
No kernel may reach another device: no remote copies, remote signals or barrier semaphores. Data moves between devices by JAX's collectives and lax.ppermute only.
A program may use at most 192 MiB of HBM per device.

v0:
```python
import jax
import jax.numpy as jnp
from jax import lax
from jax.experimental import pallas as pl
from jax.experimental.pallas import tpu as pltpu
from jax.sharding import PartitionSpec as P


TILE = 384
TASK_DEV = 64
N_MEM = 32
NX = 4
NZ = 8
RB = TILE // NZ

X_GROUPS = [[x * NZ + z for x in range(NX)] for z in range(NZ)]
Z_GROUPS = [[x * NZ + z for z in range(NZ)] for x in range(NX)]


def z_perm(step):
    return [(x * NZ + z, x * NZ + (z + step) % NZ) for x in range(NX) for z in range(NZ)]


def x_perm(step):
    return [(x * NZ + z, ((x + step) % NX) * NZ + z) for x in range(NX) for z in range(NZ)]


FIRST = (0, 1, 2, 3, 5, 6, 7)


def sum_of(keys, source, first, last, acc, unroll):
    turns = (last - first) // unroll

    def some_tasks(turn, acc):
        for u in range(unroll):
            acc = acc + source[keys[first + turn * unroll + u] & 255]
        return acc

    def one_task(t, acc):
        return acc + source[keys[t] & 255]

    acc = lax.fori_loop(0, turns, some_tasks, acc)
    return lax.fori_loop(first + turns * unroll, last, one_task, acc)


def early_kernel(keys, starts, *refs):
    ints = refs[0:7]
    mixes = refs[7:10]
    sums, wide, prod = refs[10:13]
    for k in range(7):
        wide[:, k * TILE : (k + 1) * TILE] = ints[k][...]
    for k in (0, 2, 4, 6):
        span = min(2, 7 - k)
        right = wide[:, k * TILE : (k + span) * TILE]
        for m in range(3):
            got = jnp.dot(mixes[m][...], right, preferred_element_type=jnp.float32)
            for half in range(span):
                first = (k + half) * 3 * NZ + m * NZ
                block = got[:, half * TILE : (half + 1) * TILE]
                prod[first : first + NZ] = block.reshape(NZ, RB, TILE)

    def one_output(o, carry):
        acc = jnp.zeros((RB, TILE), jnp.float32)
        sums[o] = sum_of(keys, prod, starts[2 * o], starts[2 * o + 1], acc, 4)
        return carry

    lax.fori_loop(0, N_MEM, one_output, 0)


def early(keys, starts, ints, mixes):
    smem = pl.BlockSpec(memory_space=pltpu.SMEM)
    vmem = pl.BlockSpec(memory_space=pltpu.VMEM)
    return pl.pallas_call(
        early_kernel,
        out_shape=(
            jax.ShapeDtypeStruct((N_MEM, RB, TILE), jnp.float32),
            jax.ShapeDtypeStruct((TILE, 7 * TILE), jnp.bfloat16),
        ),
        in_specs=[smem, smem] + [vmem] * 10,
        out_specs=(vmem, vmem),
        scratch_shapes=[pltpu.VMEM((7 * 3 * NZ, RB, TILE), jnp.float32)],
        compiler_params=pltpu.CompilerParams(vmem_limit_bytes=30 << 20),
    )(keys, starts, *ints, *mixes)


def late_kernel(keys, starts, last_tile, m0, m1, m2, m3, sums, wide, out, rest):
    for m, left in enumerate((m0, m1, m3, m2)):
        got = jnp.dot(left[...], last_tile[...], preferred_element_type=jnp.float32)
        rest[(7 + m) * NZ : (8 + m) * NZ] = got.reshape(NZ, RB, TILE)
    for k in (0, 2, 4, 6):
        span = min(2, 7 - k)
        right = wide[:, k * TILE : (k + span) * TILE]
        got = jnp.dot(m2[...], right, preferred_element_type=jnp.float32)
        for half in range(span):
            block = got[:, half * TILE : (half + 1) * TILE]
            rest[(k + half) * NZ : (k + half + 1) * NZ] = block.reshape(NZ, RB, TILE)

    def one_output(o, carry):
        acc = sum_of(keys, rest, starts[2 * o + 1], starts[2 * o + 2], sums[o], 2)
        out[o] = acc.astype(jnp.bfloat16)
        return carry

    lax.fori_loop(0, N_MEM, one_output, 0)


def late(keys, starts, last_tile, mixes, sums, wide):
    smem = pl.BlockSpec(memory_space=pltpu.SMEM)
    vmem = pl.BlockSpec(memory_space=pltpu.VMEM)
    return pl.pallas_call(
        late_kernel,
        out_shape=jax.ShapeDtypeStruct((N_MEM, RB, TILE), jnp.bfloat16),
        in_specs=[smem, smem] + [vmem] * 7,
        out_specs=vmem,
        scratch_shapes=[pltpu.VMEM((11 * NZ, RB, TILE), jnp.float32)],
        compiler_params=pltpu.CompilerParams(vmem_limit_bytes=24 << 20),
    )(keys, starts, last_tile, *mixes, sums, wide)


def task_keys(task_list, task_counts, owner_map, x, z):
    ids = jnp.arange(N_MEM, dtype=jnp.int32)
    hit = task_list[:, :, None] == ids[None, None, :]
    rows = jnp.sum(jnp.where(hit, owner_map[None, None, :], 0), axis=2)
    live = (jnp.arange(TASK_DEV, dtype=jnp.int32)[None, :] < task_counts[:, None]).reshape(-1)
    o, a, b = rows[:, 0], rows[:, 1], rows[:, 2]
    mine = live & ((b // NZ) == x)
    a_turn, a_row = (a // NZ - x) % NX, a % NZ
    b_slot = (b % NZ - z) % NZ
    b_rank = jnp.where(b_slot > 4, b_slot - 1, b_slot)
    a_rank = jnp.where(a_turn == 3, 2, a_turn)
    in_early = (b_slot != 4) & (a_turn != 2)
    early_at = (b_rank * 3 + a_rank) * NZ + a_row
    last_at = (7 + jnp.where(a_turn == 2, 3, a_rank)) * NZ + a_row
    late_at = 256 + jnp.where(b_slot == 4, last_at, b_rank * NZ + a_row)
    key = jnp.where(mine, o * 512 + jnp.where(in_early, early_at, late_at), 1 << 20)
    keys = lax.sort(key, is_stable=False)
    edges = jnp.arange(2 * N_MEM + 1, dtype=jnp.int32) * 256
    starts = jnp.sum((key[None, :] < edges[:, None]).astype(jnp.int32), axis=1)
    return keys, starts


def local(amplitudes, integrals, task_list, task_counts, owner_map):
    device = lax.axis_index("mem")
    x, z = device // NZ, device % NZ
    own_amp = amplitudes[0, 0]
    own_int = integrals[0, 0]

    ints = [None] * 8
    ints[0] = own_int
    fw = bw = own_int
    for step in range(1, 5):
        fw = lax.ppermute(fw, "mem", z_perm(1))
        ints[8 - step] = fw
        if step < 4:
            bw = lax.ppermute(bw, "mem", z_perm(-1))
            ints[step] = bw

    swapped = lax.all_to_all(own_amp, "grp", split_axis=0, concat_axis=0, tiled=True)
    mixed = (2.0 * own_amp.astype(jnp.float32) - swapped.astype(jnp.float32)).astype(jnp.bfloat16)
    m0 = lax.all_to_all(mixed, "mem", 0, 0, axis_index_groups=Z_GROUPS, tiled=True)
    m3 = lax.ppermute(m0, "mem", x_perm(1))
    m1 = lax.ppermute(m0, "mem", x_perm(-1))
    m2 = lax.ppermute(m3, "mem", x_perm(1))

    keys, starts = task_keys(task_list[0], task_counts[0], owner_map, x, z)
    sums, wide = early(keys, starts, [ints[slot] for slot in FIRST], (m0, m1, m3))
    part = late(keys, starts, ints[4], (m0, m1, m2, m3), sums, wide)
    got = lax.all_to_all(
        part.reshape(NX, NZ * RB, TILE), "mem", 0, 0, axis_index_groups=X_GROUPS, tiled=True
    )
    summed = jnp.sum(got.astype(jnp.float32), axis=0).astype(jnp.bfloat16)
    out = lax.all_to_all(summed, "mem", 0, 0, axis_index_groups=Z_GROUPS, tiled=True)
    return out[None, None]


def solution(mesh):
    placed = (
        P("grp", "mem", None, None),
        P("grp", "mem", None, None),
        P("grp", None, None),
        P("grp", None),
        P(),
    )
    return jax.shard_map(
        local, mesh=mesh, in_specs=placed, out_specs=P("grp", "mem", None, None), check_vma=False
    )
```

profile of v0, /device:TPU:8, one launch (start us, length us, event | category | flops | bytes accessed | tf_op | source)
XLA Modules:
  0.0 102.8 jit_solution(12027622630219288712)
XLA Ops:
  0.0 0.0 copy-start
  0.0 0.0 copy-start.1
  0.0 0.0 copy-start.3
  0.0 0.0 copy-start.2
  0.0 5.6 %all-to-all-start = ((bf16[8,48,384]{2,1,0:T(8,128)(2,1)}), bf16[8,48,384]{2,1,0:T(8,128)(2,1)S(1)}, u32[]{:S(2)}, u32[]{:S(2)}) async-start(bf16[8,48,384]{2,1,0:T(8,128)(2,1)} %bitcast.21), calls=%async_computation | async-start | bytes 589824 | tf_op jit(solution)/shard_map/all_to_all | solution.py:157
  5.6 1.4 %collective-permute-start = (bf16[384,384]{1,0:T(8,128)(2,1)}, bf16[384,384]{1,0:T(8,128)(2,1)S(1)}, u32[]{:S(2)}, u32[]{:S(2)}) collective-permute-start(bf16[384,384]{1,0:T(8,128)(2,1)} %bitcast.18), channel_id=1, source_target_pairs={{0,1},{1,2},{2,3},{3,4},{4,5},{5,6},{6,7},{7,0},{8,9},{9,10},{10,1... | collective-permute-start | bytes 884744 | tf_op jit(solution)/shard_map/ppermute | solution.py:151
  7.0 5.1 %all-to-all-done = bf16[8,48,384]{2,1,0:T(8,128)(2,1)S(1)} async-done(((bf16[8,48,384]{2,1,0:T(8,128)(2,1)}), bf16[8,48,384]{2,1,0:T(8,128)(2,1)S(1)}, u32[]{:S(2)}, u32[]{:S(2)}) %all-to-all-start) | async-done | bytes 294944 | tf_op jit(solution)/shard_map/all_to_all | solution.py:157
  12.1 1.8 %subtract_convert_fusion = bf16[8,48,384]{2,1,0:T(8,128)(2,1)} fusion(bf16[8,48,384]{2,1,0:T(8,128)(2,1)S(1)} %all-to-all-done, bf16[8,48,384]{2,1,0:T(8,128)(2,1)} %bitcast.22), kind=kLoop, calls=%fused_computation.2 | loop fusion | flops 737280 | bytes 884736 | tf_op jit(solution)/shard_map/convert_element_type | solution.py:158
  13.8 7.9 %all-to-all-start.1 = ((bf16[8,48,384]{2,1,0:T(8,128)(2,1)}), bf16[8,48,384]{2,1,0:T(8,128)(2,1)S(1)}, u32[]{:S(2)}, u32[]{:S(2)}) async-start(bf16[8,48,384]{2,1,0:T(8,128)(2,1)} %subtract_convert_fusion), calls=%async_computation.1 | async-start | bytes 589824 | tf_op jit(solution)/shard_map/all_to_all | solution.py:159
  21.7 0.0 copy-done
  21.7 3.2 %collective-permute-start.7 = (bf16[384,384]{1,0:T(8,128)(2,1)S(1)}, bf16[384,384]{1,0:T(8,128)(2,1)S(1)}, u32[]{:S(2)}, u32[]{:S(2)}) collective-permute-start(bf16[384,384]{1,0:T(8,128)(2,1)S(1)} %bitcast.19), channel_id=1, source_target_pairs={{0,7},{1,0},{2,1},{3,2},{4,3},{5,4},{6,5},{7,6},{8,15},{9,8},{10,9... | collective-permute-start | bytes 884744 | tf_op jit(solution)/shard_map/ppermute | solution.py:154
  25.0 0.0 copy-done.1
  25.0 0.0 collective-permute-done.refs_6_
  25.0 0.1 collective-permute-start.1
  25.1 0.0 copy-done.3
  25.1 0.1 iota_compare_fusion.1
  25.2 0.1 lt.64
  25.2 0.0 copy-done.2
  25.2 0.2 select_reduce_fusion
  25.5 11.1 %collective-permute-done.7.refs_1_ = bf16[384,384]{1,0:T(8,128)(2,1)S(1)} collective-permute-done((bf16[384,384]{1,0:T(8,128)(2,1)S(1)}, bf16[384,384]{1,0:T(8,128)(2,1)S(1)}, u32[]{:S(2)}, u32[]{:S(2)}) %collective-permute-start.7) | collective-permute-done | bytes 294944 | tf_op jit(solution)/shard_map/ppermute | solution.py:154
  36.6 1.6 %collective-permute-start.8 = (bf16[384,384]{1,0:T(8,128)(2,1)S(1)}, bf16[384,384]{1,0:T(8,128)(2,1)S(1)}, u32[]{:S(2)}, u32[]{:S(2)}) collective-permute-start(bf16[384,384]{1,0:T(8,128)(2,1)S(1)} %collective-permute-done.7.refs_1_), channel_id=1, source_target_pairs={{0,7},{1,0},{2,1},{3,2},{4,3},{5,4},{6,5},{7,6},{8,15},{9,8},{10,9... | collective-permute-start | bytes 884744 | tf_op jit(solution)/shard_map/ppermute | solution.py:154
  38.1 0.0 collective-permute-done.1.refs_5_
  38.2 0.5 collective-permute-start.2
  38.6 0.0 all-to-all-done.1
  38.6 1.5 %collective-permute-start.5 = (bf16[384,384]{1,0:T(8,128)(2,1)S(1)}, bf16[384,384]{1,0:T(8,128)(2,1)S(1)}, u32[]{:S(2)}, u32[]{:S(2)}) collective-permute-start(bf16[384,384]{1,0:T(8,128)(2,1)S(1)} %bitcast.14), channel_id=1, source_target_pairs={{0,8},{1,9},{2,10},{3,11},{4,12},{5,13},{6,14},{7,15},{8,16},{9,17... | collective-permute-start | bytes 884744 | tf_op jit(solution)/shard_map/ppermute | solution.py:160
  40.1 4.1 %collective-permute-done.8.refs_2_ = bf16[384,384]{1,0:T(8,128)(2,1)S(1)} collective-permute-done((bf16[384,384]{1,0:T(8,128)(2,1)S(1)}, bf16[384,384]{1,0:T(8,128)(2,1)S(1)}, u32[]{:S(2)}, u32[]{:S(2)}) %collective-permute-start.8) | collective-permute-done | bytes 294944 | tf_op jit(solution)/shard_map/ppermute | solution.py:154
  44.2 3.4 %collective-permute-start.9 = (bf16[384,384]{1,0:T(8,128)(2,1)S(1)}, bf16[384,384]{1,0:T(8,128)(2,1)S(1)}, u32[]{:S(2)}, u32[]{:S(2)}) collective-permute-start(bf16[384,384]{1,0:T(8,128)(2,1)S(1)} %collective-permute-done.8.refs_2_), channel_id=1, source_target_pairs={{0,7},{1,0},{2,1},{3,2},{4,3},{5,4},{6,5},{7,6},{8,15},{9,8},{10,9... | collective-permute-start | bytes 884744 | tf_op jit(solution)/shard_map/ppermute | solution.py:154
  47.6 2.8 %collective-permute-start.4 = (bf16[384,384]{1,0:T(8,128)(2,1)S(1)}, bf16[384,384]{1,0:T(8,128)(2,1)S(1)}, u32[]{:S(2)}, u32[]{:S(2)}) collective-permute-start(bf16[384,384]{1,0:T(8,128)(2,1)S(1)} %bitcast.15), channel_id=1, source_target_pairs={{0,24},{1,25},{2,26},{3,27},{4,28},{5,29},{6,30},{7,31},{8,0},{9,1... | collective-permute-start | bytes 884744 | tf_op jit(solution)/shard_map/ppermute | solution.py:161
  50.4 0.0 collective-permute-done.2.refs_4_
  50.4 0.0 collective-permute-start.3
  50.4 0.0 collective-permute-done.5.refs_9_.m3
  50.4 0.3 collective-permute-start.6
  50.7 4.3 %sort.7.keys = s32[2048]{0:T(1024)S(1)} sort(s32[2048]{0:T(1024)S(1)} %add_select_fusion.6), dimensions={0}, to_apply=%region_1.2 | sort | flops 22528 | bytes 16384 | tf_op jit(solution)/shard_map/sort | solution.py:135
  55.0 0.2 convert_reduce_fusion.starts
  55.2 0.0 collective-permute-done.9.refs_3_
  55.2 0.0 collective-permute-done.4.refs_8_.m1
  55.2 6.4 %shard_map.55 = (f32[32,48,384]{2,1,0:T(8,128)S(1)}, bf16[384,2688]{1,0:T(8,128)(2,1)S(1)}) custom-call(s32[2048]{0:T(1024)S(1)} %sort.7.keys, s32[65]{0:T(128)S(1)} %convert_reduce_fusion.starts, bf16[384,384]{1,0:T(8,128)(2,1)S(1)} %bitcast.20, bf16[384,384]{1,0:T(8,128)(2,1)S(1)} %collective-permute-done.7.refs_1_, ...), custom_call_target="tpu_custom_call" | custom-call | tf_op jit(solution)/shard_map/pallas_call | solution.py:73
  61.6 0.0 collective-permute-done.3.last_tile
  61.6 0.0 collective-permute-done.6.m2
  61.6 4.2 %shard_map.56 = bf16[32,48,384]{2,1,0:T(8,128)(2,1)S(1)} custom-call(s32[2048]{0:T(1024)S(1)} %sort.7.keys, s32[65]{0:T(128)S(1)} %convert_reduce_fusion.starts, bf16[384,384]{1,0:T(8,128)(2,1)S(1)} %collective-permute-done.3.last_tile, bf16[384,384]{1,0:T(8,128)(2,1)S(1)} %bitcast.17, bf16[384,384]{1,0:T(8,128)(2,1)S(1)} %collective-permute-done.4.refs_8_.m1, ...), custom_call_target="tpu_custom_call" | custom-call | tf_op jit(solution)/shard_map/pallas_call | solution.py:109
  65.8 18.5 %all_to_all.28 = bf16[4,384,384]{2,1,0:T(8,128)(2,1)S(1)} all-to-all(bf16[4,384,384]{2,1,0:T(8,128)(2,1)S(1)} %bitcast.13), channel_id=1, replica_groups={{0,8,16,24},{1,9,17,25},{2,10,18,26},{3,11,19,27},{4,12,20,28},{5,13,21..., dimensions={0} | all-to-all | bytes 2359296 | tf_op jit(solution)/shard_map/all_to_all | solution.py:167
  84.3 0.3 reduce_sum.32
  84.6 17.5 %all_to_all.29 = bf16[8,48,384]{2,1,0:T(8,128)(2,1)S(1)} all-to-all(bf16[8,48,384]{2,1,0:T(8,128)(2,1)S(1)} %bitcast.24), channel_id=1, replica_groups={{0,1,2,3,4,5,6,7},{8,9,10,11,12,13,14,15},{16,17,18,19,20,21,22,23},{24..., dimensions={0} | all-to-all | bytes 589824 | tf_op jit(solution)/shard_map/all_to_all | solution.py:171
  102.1 0.7 copy.12
  (4 shorter events, 0.1 us)
Async XLA Ops:
  0.0 21.7 %copy-start = (bf16[1,1,384,384]{3,2,1,0:T(8,128)(2,1)S(1)}, bf16[1,1,384,384]{3,2,1,0:T(8,128)(2,1)}, u32[]{:S(2)}) copy-start(bf16[1,1,384,384]{3,2,1,0:T(8,128)(2,1)} %param.6) | copy-start | bytes 884740
  0.0 25.0 %copy-start.1 = (s32[1,2048,3]{1,0,2:T(1,128)S(1)}, s32[1,2048,3]{1,0,2:T(1,128)}, u32[]{:S(2)}) copy-start(s32[1,2048,3]{1,0,2:T(1,128)} %param.7) | copy-start | bytes 73732
  0.0 25.1 %copy-start.3 = (s32[1,32]{1,0:T(1,128)S(1)}, s32[1,32]{1,0:T(1,128)}, u32[]{:S(2)}) copy-start(s32[1,32]{1,0:T(1,128)} %param.8) | copy-start | bytes 388
  0.0 25.2 %copy-start.2 = (s32[32]{0:T(128)S(1)}, s32[32]{0:T(128)}, u32[]{:S(2)}) copy-start(s32[32]{0:T(128)} %param.9) | copy-start | bytes 388
  0.0 12.0 %all-to-all-start = ((bf16[8,48,384]{2,1,0:T(8,128)(2,1)}), bf16[8,48,384]{2,1,0:T(8,128)(2,1)S(1)}, u32[]{:S(2)}, u32[]{:S(2)}) async-start(bf16[8,48,384]{2,1,0:T(8,128)(2,1)} %bitcast.21), calls=%async_computation | async-start | bytes 589824 | tf_op jit(solution)/shard_map/all_to_all | solution.py:157
  5.6 19.3 %collective-permute-start = (bf16[384,384]{1,0:T(8,128)(2,1)}, bf16[384,384]{1,0:T(8,128)(2,1)S(1)}, u32[]{:S(2)}, u32[]{:S(2)}) collective-permute-start(bf16[384,384]{1,0:T(8,128)(2,1)} %bitcast.18), channel_id=1, source_target_pairs={{0,1},{1,2},{2,3},{3,4},{4,5},{5,6},{6,7},{7,0},{8,9},{9,10},{10,1... | collective-permute-start | bytes 884744 | tf_op jit(solution)/shard_map/ppermute | solution.py:151
  13.8 24.8 %all-to-all-start.1 = ((bf16[8,48,384]{2,1,0:T(8,128)(2,1)}), bf16[8,48,384]{2,1,0:T(8,128)(2,1)S(1)}, u32[]{:S(2)}, u32[]{:S(2)}) async-start(bf16[8,48,384]{2,1,0:T(8,128)(2,1)} %subtract_convert_fusion), calls=%async_computation.1 | async-start | bytes 589824 | tf_op jit(solution)/shard_map/all_to_all | solution.py:159
  21.7 14.9 %collective-permute-start.7 = (bf16[384,384]{1,0:T(8,128)(2,1)S(1)}, bf16[384,384]{1,0:T(8,128)(2,1)S(1)}, u32[]{:S(2)}, u32[]{:S(2)}) collective-permute-start(bf16[384,384]{1,0:T(8,128)(2,1)S(1)} %bitcast.19), channel_id=1, source_target_pairs={{0,7},{1,0},{2,1},{3,2},{4,3},{5,4},{6,5},{7,6},{8,15},{9,8},{10,9... | collective-permute-start | bytes 884744 | tf_op jit(solution)/shard_map/ppermute | solution.py:154
  25.0 13.2 %collective-permute-start.1 = (bf16[384,384]{1,0:T(8,128)(2,1)S(1)}, bf16[384,384]{1,0:T(8,128)(2,1)S(1)}, u32[]{:S(2)}, u32[]{:S(2)}) collective-permute-start(bf16[384,384]{1,0:T(8,128)(2,1)S(1)} %collective-permute-done.refs_6_), channel_id=1, source_target_pairs={{0,1},{1,2},{2,3},{3,4},{4,5},{5,6},{6,7},{7,0},{8,9},{9,10},{10,1... | collective-permute-start | bytes 884744 | tf_op jit(solution)/shard_map/ppermute | solution.py:151
  36.6 7.6 %collective-permute-start.8 = (bf16[384,384]{1,0:T(8,128)(2,1)S(1)}, bf16[384,384]{1,0:T(8,128)(2,1)S(1)}, u32[]{:S(2)}, u32[]{:S(2)}) collective-permute-start(bf16[384,384]{1,0:T(8,128)(2,1)S(1)} %collective-permute-done.7.refs_1_), channel_id=1, source_target_pairs={{0,7},{1,0},{2,1},{3,2},{4,3},{5,4},{6,5},{7,6},{8,15},{9,8},{10,9... | collective-permute-start | bytes 884744 | tf_op jit(solution)/shard_map/ppermute | solution.py:154
  38.2 12.2 %collective-permute-start.2 = (bf16[384,384]{1,0:T(8,128)(2,1)S(1)}, bf16[384,384]{1,0:T(8,128)(2,1)S(1)}, u32[]{:S(2)}, u32[]{:S(2)}) collective-permute-start(bf16[384,384]{1,0:T(8,128)(2,1)S(1)} %collective-permute-done.1.refs_5_), channel_id=1, source_target_pairs={{0,1},{1,2},{2,3},{3,4},{4,5},{5,6},{6,7},{7,0},{8,9},{9,10},{10,1... | collective-permute-start | bytes 884744 | tf_op jit(solution)/shard_map/ppermute | solution.py:151
  38.6 11.8 %collective-permute-start.5 = (bf16[384,384]{1,0:T(8,128)(2,1)S(1)}, bf16[384,384]{1,0:T(8,128)(2,1)S(1)}, u32[]{:S(2)}, u32[]{:S(2)}) collective-permute-start(bf16[384,384]{1,0:T(8,128)(2,1)S(1)} %bitcast.14), channel_id=1, source_target_pairs={{0,8},{1,9},{2,10},{3,11},{4,12},{5,13},{6,14},{7,15},{8,16},{9,17... | collective-permute-start | bytes 884744 | tf_op jit(solution)/shard_map/ppermute | solution.py:160
  44.2 11.0 %collective-permute-start.9 = (bf16[384,384]{1,0:T(8,128)(2,1)S(1)}, bf16[384,384]{1,0:T(8,128)(2,1)S(1)}, u32[]{:S(2)}, u32[]{:S(2)}) collective-permute-start(bf16[384,384]{1,0:T(8,128)(2,1)S(1)} %collective-permute-done.8.refs_2_), channel_id=1, source_target_pairs={{0,7},{1,0},{2,1},{3,2},{4,3},{5,4},{6,5},{7,6},{8,15},{9,8},{10,9... | collective-permute-start | bytes 884744 | tf_op jit(solution)/shard_map/ppermute | solution.py:154
  47.6 7.6 %collective-permute-start.4 = (bf16[384,384]{1,0:T(8,128)(2,1)S(1)}, bf16[384,384]{1,0:T(8,128)(2,1)S(1)}, u32[]{:S(2)}, u32[]{:S(2)}) collective-permute-start(bf16[384,384]{1,0:T(8,128)(2,1)S(1)} %bitcast.15), channel_id=1, source_target_pairs={{0,24},{1,25},{2,26},{3,27},{4,28},{5,29},{6,30},{7,31},{8,0},{9,1... | collective-permute-start | bytes 884744 | tf_op jit(solution)/shard_map/ppermute | solution.py:161
  50.4 11.2 %collective-permute-start.3 = (bf16[384,384]{1,0:T(8,128)(2,1)S(1)}, bf16[384,384]{1,0:T(8,128)(2,1)S(1)}, u32[]{:S(2)}, u32[]{:S(2)}) collective-permute-start(bf16[384,384]{1,0:T(8,128)(2,1)S(1)} %collective-permute-done.2.refs_4_), channel_id=1, source_target_pairs={{0,1},{1,2},{2,3},{3,4},{4,5},{5,6},{6,7},{7,0},{8,9},{9,10},{10,1... | collective-permute-start | bytes 884744 | tf_op jit(solution)/shard_map/ppermute | solution.py:151
  50.4 11.2 %collective-permute-start.6 = (bf16[384,384]{1,0:T(8,128)(2,1)S(1)}, bf16[384,384]{1,0:T(8,128)(2,1)S(1)}, u32[]{:S(2)}, u32[]{:S(2)}) collective-permute-start(bf16[384,384]{1,0:T(8,128)(2,1)S(1)} %collective-permute-done.5.refs_9_.m3), channel_id=1, source_target_pairs={{0,8},{1,9},{2,10},{3,11},{4,12},{5,13},{6,14},{7,15},{8,16},{9,17... | collective-permute-start | bytes 884744 | tf_op jit(solution)/shard_map/ppermute | solution.py:162
where the time goes:
time: 103 us
  blocking collectives  36 us (35%)
  starting transfers between devices  28.1 us (27%)
  waiting for transfers between devices  20.3 us (20%)
  Pallas kernels  10.6 us (10%)
  other arithmetic  6.91 us (7%)
    all_to_all x1, blocking collectives, local(): lax.all_to_all(part.reshape(NX, NZ * RB, TILE), 'mem', 0, 0, axis_index_g...  18.5 us
    all_to_all x1, blocking collectives, local(): lax.all_to_all(summed, 'mem', 0, 0, axis_index_groups=Z_GROUPS, tiled=True)  17.5 us
    ppermute x3, waiting for transfers between devices, local(): bw = lax.ppermute(bw, 'mem', z_perm(-1))  15.2 us
    ppermute x3, starting transfers between devices, local(): bw = lax.ppermute(bw, 'mem', z_perm(-1))  8.19 us
    all_to_all x1, starting transfers between devices, local(): lax.all_to_all(mixed, 'mem', 0, 0, axis_index_groups=Z_GROUPS, tiled=True)  7.88 us
    pallas_call x1, Pallas kernels, early(): pl.pallas_call(early_kernel, out_shape=(jax.ShapeDtypeStruct((N_MEM, RB,...  6.37 us
    all_to_all x1, starting transfers between devices, local(): lax.all_to_all(own_amp, 'grp', split_axis=0, concat_axis=0, tiled=True)  5.61 us
    all_to_all x1, waiting for transfers between devices, local(): lax.all_to_all(own_amp, 'grp', split_axis=0, concat_axis=0, tiled=True)  5.07 us
  transfers between devices with their start and end apart: 12, of which 3 were waited for; matrix products, arithmetic and copies ran while one was open for 7% of the time, Pallas kernels for 6%

commit v1 on v0

--- a/solution.py
+++ b/solution.py
@@ -96,7 +96,12 @@
             rest[(k + half) * NZ : (k + half + 1) * NZ] = block.reshape(NZ, RB, TILE)
 
     def one_output(o, carry):
-        acc = sum_of(keys, rest, starts[2 * o + 1], starts[2 * o + 2], sums[o], 2)
+        acc = lax.fori_loop(
+            starts[2 * o + 1],
+            starts[2 * o + 2],
+            lambda t, acc: acc + rest[keys[t] & 255],
+            sums[o],
+        )
         out[o] = acc.astype(jnp.bfloat16)
         return carry
 
@@ -154,8 +159,9 @@
             bw = lax.ppermute(bw, "mem", z_perm(-1))
             ints[step] = bw
 
+    doubled = lax.optimization_barrier(2.0 * own_amp.astype(jnp.float32))
     swapped = lax.all_to_all(own_amp, "grp", split_axis=0, concat_axis=0, tiled=True)
-    mixed = (2.0 * own_amp.astype(jnp.float32) - swapped.astype(jnp.float32)).astype(jnp.bfloat16)
+    mixed = (doubled - swapped.astype(jnp.float32)).astype(jnp.bfloat16)
     m0 = lax.all_to_all(mixed, "mem", 0, 0, axis_index_groups=Z_GROUPS, tiled=True)
     m3 = lax.ppermute(m0, "mem", x_perm(1))
     m1 = lax.ppermute(m0, "mem", x_perm(-1))

time: 103 us -> 102 us (level)
  no operation moved by 1% of the time
where the time goes in v1:
time: 102 us
  blocking collectives  36 us (35%)
  starting transfers between devices  28.1 us (28%)
  waiting for transfers between devices  19.3 us (19%)
  Pallas kernels  10.4 us (10%)
  other arithmetic  6.96 us (7%)
    all_to_all x1, blocking collectives, local(): lax.all_to_all(part.reshape(NX, NZ * RB, TILE), 'mem', 0, 0, axis_index_g...  18.5 us
    all_to_all x1, blocking collectives, local(): lax.all_to_all(summed, 'mem', 0, 0, axis_index_groups=Z_GROUPS, tiled=True)  17.5 us
    ppermute x3, waiting for transfers between devices, local(): bw = lax.ppermute(bw, 'mem', z_perm(-1))  15.2 us
    ppermute x3, starting transfers between devices, local(): bw = lax.ppermute(bw, 'mem', z_perm(-1))  8.19 us
    all_to_all x1, starting transfers between devices, local(): lax.all_to_all(mixed, 'mem', 0, 0, axis_index_groups=Z_GROUPS, tiled=True)  7.88 us
    pallas_call x1, Pallas kernels, early(): pl.pallas_call(early_kernel, out_shape=(jax.ShapeDtypeStruct((N_MEM, RB,...  6.37 us
    all_to_all x1, starting transfers between devices, local(): lax.all_to_all(own_amp, 'grp', split_axis=0, concat_axis=0, tiled=True)  5.61 us
    sort x1, other arithmetic, task_keys(): keys = lax.sort(key, is_stable=False)  4.26 us
  transfers between devices with their start and end apart: 12, of which 3 were waited for; matrix products, arithmetic and copies ran while one was open for 7% of the time, Pallas kernels for 6%

profile of v1, /device:TPU:8, one launch (start us, length us, event | category | flops | bytes accessed | tf_op | source)
XLA Modules:
  0.0 101.8 jit_solution(692008596878582666)
XLA Ops:
  0.0 0.0 copy-start
  0.0 0.0 copy-start.1
  0.0 0.0 copy-start.3
  0.0 0.0 copy-start.2
  0.0 5.6 %all-to-all-start = ((bf16[8,48,384]{2,1,0:T(8,128)(2,1)}), bf16[8,48,384]{2,1,0:T(8,128)(2,1)S(1)}, u32[]{:S(2)}, u32[]{:S(2)}) async-start(bf16[8,48,384]{2,1,0:T(8,128)(2,1)} %bitcast.27), calls=%async_computation | async-start | bytes 589824 | tf_op jit(solution)/shard_map/all_to_all | solution.py:163
  5.6 1.4 %collective-permute-start = (bf16[384,384]{1,0:T(8,128)(2,1)}, bf16[384,384]{1,0:T(8,128)(2,1)S(1)}, u32[]{:S(2)}, u32[]{:S(2)}) collective-permute-start(bf16[384,384]{1,0:T(8,128)(2,1)} %bitcast.24), channel_id=1, source_target_pairs={{0,1},{1,2},{2,3},{3,4},{4,5},{5,6},{6,7},{7,0},{8,9},{9,10},{10,1... | collective-permute-start | bytes 884744 | tf_op jit(solution)/shard_map/ppermute | solution.py:156
  7.0 1.0 multiply_bitcast_fusion
  8.0 4.1 %all-to-all-done = bf16[8,48,384]{2,1,0:T(8,128)(2,1)S(1)} async-done(((bf16[8,48,384]{2,1,0:T(8,128)(2,1)}), bf16[8,48,384]{2,1,0:T(8,128)(2,1)S(1)}, u32[]{:S(2)}, u32[]{:S(2)}) %all-to-all-start) | async-done | bytes 294944 | tf_op jit(solution)/shard_map/all_to_all | solution.py:163
  12.1 0.8 fusion
  12.9 7.9 %all-to-all-start.1 = ((bf16[8,48,384]{2,1,0:T(8,128)(2,1)}), bf16[8,48,384]{2,1,0:T(8,128)(2,1)S(1)}, u32[]{:S(2)}, u32[]{:S(2)}) async-start(bf16[8,48,384]{2,1,0:T(8,128)(2,1)} %bitcast.8), calls=%async_computation.1 | async-start | bytes 589824 | tf_op jit(solution)/shard_map/all_to_all | solution.py:165
  20.8 0.0 copy-done
  20.8 3.2 %collective-permute-start.7 = (bf16[384,384]{1,0:T(8,128)(2,1)S(1)}, bf16[384,384]{1,0:T(8,128)(2,1)S(1)}, u32[]{:S(2)}, u32[]{:S(2)}) collective-permute-start(bf16[384,384]{1,0:T(8,128)(2,1)S(1)} %bitcast.25), channel_id=1, source_target_pairs={{0,7},{1,0},{2,1},{3,2},{4,3},{5,4},{6,5},{7,6},{8,15},{9,8},{10,9... | collective-permute-start | bytes 884744 | tf_op jit(solution)/shard_map/ppermute | solution.py:159
  24.0 0.0 copy-done.1
  24.0 0.0 collective-permute-done.refs_6_
  24.0 0.1 collective-permute-start.1
  24.1 0.0 copy-done.3
  24.1 0.1 iota_compare_fusion.1
  24.2 0.1 lt.64
  24.3 0.0 copy-done.2
  24.3 0.2 select_reduce_fusion
  24.5 11.1 %collective-permute-done.7.refs_1_ = bf16[384,384]{1,0:T(8,128)(2,1)S(1)} collective-permute-done((bf16[384,384]{1,0:T(8,128)(2,1)S(1)}, bf16[384,384]{1,0:T(8,128)(2,1)S(1)}, u32[]{:S(2)}, u32[]{:S(2)}) %collective-permute-start.7) | collective-permute-done | bytes 294944 | tf_op jit(solution)/shard_map/ppermute | solution.py:159
  35.6 1.6 %collective-permute-start.8 = (bf16[384,384]{1,0:T(8,128)(2,1)S(1)}, bf16[384,384]{1,0:T(8,128)(2,1)S(1)}, u32[]{:S(2)}, u32[]{:S(2)}) collective-permute-start(bf16[384,384]{1,0:T(8,128)(2,1)S(1)} %collective-permute-done.7.refs_1_), channel_id=1, source_target_pairs={{0,7},{1,0},{2,1},{3,2},{4,3},{5,4},{6,5},{7,6},{8,15},{9,8},{10,9... | collective-permute-start | bytes 884744 | tf_op jit(solution)/shard_map/ppermute | solution.py:159
  37.2 0.0 collective-permute-done.1.refs_5_
  37.2 0.5 collective-permute-start.2
  37.7 0.0 all-to-all-done.1
  37.7 1.5 %collective-permute-start.5 = (bf16[384,384]{1,0:T(8,128)(2,1)S(1)}, bf16[384,384]{1,0:T(8,128)(2,1)S(1)}, u32[]{:S(2)}, u32[]{:S(2)}) collective-permute-start(bf16[384,384]{1,0:T(8,128)(2,1)S(1)} %bitcast.20), channel_id=1, source_target_pairs={{0,8},{1,9},{2,10},{3,11},{4,12},{5,13},{6,14},{7,15},{8,16},{9,17... | collective-permute-start | bytes 884744 | tf_op jit(solution)/shard_map/ppermute | solution.py:166
  39.2 4.1 %collective-permute-done.8.refs_2_ = bf16[384,384]{1,0:T(8,128)(2,1)S(1)} collective-permute-done((bf16[384,384]{1,0:T(8,128)(2,1)S(1)}, bf16[384,384]{1,0:T(8,128)(2,1)S(1)}, u32[]{:S(2)}, u32[]{:S(2)}) %collective-permute-start.8) | collective-permute-done | bytes 294944 | tf_op jit(solution)/shard_map/ppermute | solution.py:159
  43.3 3.4 %collective-permute-start.9 = (bf16[384,384]{1,0:T(8,128)(2,1)S(1)}, bf16[384,384]{1,0:T(8,128)(2,1)S(1)}, u32[]{:S(2)}, u32[]{:S(2)}) collective-permute-start(bf16[384,384]{1,0:T(8,128)(2,1)S(1)} %collective-permute-done.8.refs_2_), channel_id=1, source_target_pairs={{0,7},{1,0},{2,1},{3,2},{4,3},{5,4},{6,5},{7,6},{8,15},{9,8},{10,9... | collective-permute-start | bytes 884744 | tf_op jit(solution)/shard_map/ppermute | solution.py:159
  46.7 2.8 %collective-permute-start.4 = (bf16[384,384]{1,0:T(8,128)(2,1)S(1)}, bf16[384,384]{1,0:T(8,128)(2,1)S(1)}, u32[]{:S(2)}, u32[]{:S(2)}) collective-permute-start(bf16[384,384]{1,0:T(8,128)(2,1)S(1)} %bitcast.21), channel_id=1, source_target_pairs={{0,24},{1,25},{2,26},{3,27},{4,28},{5,29},{6,30},{7,31},{8,0},{9,1... | collective-permute-start | bytes 884744 | tf_op jit(solution)/shard_map/ppermute | solution.py:167
  49.4 0.0 collective-permute-done.2.refs_4_
  49.4 0.0 collective-permute-start.3
  49.4 0.0 collective-permute-done.5.refs_9_.m3
  49.4 0.3 collective-permute-start.6
  49.8 4.3 %sort.7.keys = s32[2048]{0:T(1024)S(1)} sort(s32[2048]{0:T(1024)S(1)} %add_select_fusion.6), dimensions={0}, to_apply=%region_1.2 | sort | flops 22528 | bytes 16384 | tf_op jit(solution)/shard_map/sort | solution.py:140
  54.0 0.2 convert_reduce_fusion.starts
  54.3 0.0 collective-permute-done.9.refs_3_
  54.3 0.0 collective-permute-done.4.refs_8_.m1
  54.3 6.4 %shard_map.55 = (f32[32,48,384]{2,1,0:T(8,128)S(1)}, bf16[384,2688]{1,0:T(8,128)(2,1)S(1)}) custom-call(s32[2048]{0:T(1024)S(1)} %sort.7.keys, s32[65]{0:T(128)S(1)} %convert_reduce_fusion.starts, bf16[384,384]{1,0:T(8,128)(2,1)S(1)} %bitcast.26, bf16[384,384]{1,0:T(8,128)(2,1)S(1)} %collective-permute-done.7.refs_1_, ...), custom_call_target="tpu_custom_call" | custom-call | tf_op jit(solution)/shard_map/pallas_call | solution.py:73
  60.7 0.0 collective-permute-done.3.last_tile
  60.7 0.0 collective-permute-done.6.m2
  60.7 4.1 %shard_map.56 = bf16[32,48,384]{2,1,0:T(8,128)(2,1)S(1)} custom-call(s32[2048]{0:T(1024)S(1)} %sort.7.keys, s32[65]{0:T(128)S(1)} %convert_reduce_fusion.starts, bf16[384,384]{1,0:T(8,128)(2,1)S(1)} %collective-permute-done.3.last_tile, bf16[384,384]{1,0:T(8,128)(2,1)S(1)} %bitcast.23, bf16[384,384]{1,0:T(8,128)(2,1)S(1)} %collective-permute-done.4.refs_8_.m1, ...), custom_call_target="tpu_custom_call" | custom-call | tf_op jit(solution)/shard_map/pallas_call | solution.py:114
  64.8 18.5 %all_to_all.34 = bf16[4,384,384]{2,1,0:T(8,128)(2,1)S(1)} all-to-all(bf16[4,384,384]{2,1,0:T(8,128)(2,1)S(1)} %bitcast.19), channel_id=1, replica_groups={{0,8,16,24},{1,9,17,25},{2,10,18,26},{3,11,19,27},{4,12,20,28},{5,13,21..., dimensions={0} | all-to-all | bytes 2359296 | tf_op jit(solution)/shard_map/all_to_all | solution.py:173
  83.3 0.3 reduce_sum.32
  83.6 17.5 %all_to_all.35 = bf16[8,48,384]{2,1,0:T(8,128)(2,1)S(1)} all-to-all(bf16[8,48,384]{2,1,0:T(8,128)(2,1)S(1)} %bitcast.29), channel_id=1, replica_groups={{0,1,2,3,4,5,6,7},{8,9,10,11,12,13,14,15},{16,17,18,19,20,21,22,23},{24..., dimensions={0} | all-to-all | bytes 589824 | tf_op jit(solution)/shard_map/all_to_all | solution.py:177
  101.1 0.7 copy.12
  (4 shorter events, 0.1 us)
Async XLA Ops:
  0.0 20.8 %copy-start = (bf16[1,1,384,384]{3,2,1,0:T(8,128)(2,1)S(1)}, bf16[1,1,384,384]{3,2,1,0:T(8,128)(2,1)}, u32[]{:S(2)}) copy-start(bf16[1,1,384,384]{3,2,1,0:T(8,128)(2,1)} %param.6) | copy-start | bytes 884740
  0.0 24.0 %copy-start.1 = (s32[1,2048,3]{1,0,2:T(1,128)S(1)}, s32[1,2048,3]{1,0,2:T(1,128)}, u32[]{:S(2)}) copy-start(s32[1,2048,3]{1,0,2:T(1,128)} %param.7) | copy-start | bytes 73732
  0.0 24.1 %copy-start.3 = (s32[1,32]{1,0:T(1,128)S(1)}, s32[1,32]{1,0:T(1,128)}, u32[]{:S(2)}) copy-start(s32[1,32]{1,0:T(1,128)} %param.8) | copy-start | bytes 388
  0.0 24.3 %copy-start.2 = (s32[32]{0:T(128)S(1)}, s32[32]{0:T(128)}, u32[]{:S(2)}) copy-start(s32[32]{0:T(128)} %param.9) | copy-start | bytes 388
  0.0 12.0 %all-to-all-start = ((bf16[8,48,384]{2,1,0:T(8,128)(2,1)}), bf16[8,48,384]{2,1,0:T(8,128)(2,1)S(1)}, u32[]{:S(2)}, u32[]{:S(2)}) async-start(bf16[8,48,384]{2,1,0:T(8,128)(2,1)} %bitcast.27), calls=%async_computation | async-start | bytes 589824 | tf_op jit(solution)/shard_map/all_to_all | solution.py:163
  5.6 18.4 %collective-permute-start = (bf16[384,384]{1,0:T(8,128)(2,1)}, bf16[384,384]{1,0:T(8,128)(2,1)S(1)}, u32[]{:S(2)}, u32[]{:S(2)}) collective-permute-start(bf16[384,384]{1,0:T(8,128)(2,1)} %bitcast.24), channel_id=1, source_target_pairs={{0,1},{1,2},{2,3},{3,4},{4,5},{5,6},{6,7},{7,0},{8,9},{9,10},{10,1... | collective-permute-start | bytes 884744 | tf_op jit(solution)/shard_map/ppermute | solution.py:156
  12.9 24.8 %all-to-all-start.1 = ((bf16[8,48,384]{2,1,0:T(8,128)(2,1)}), bf16[8,48,384]{2,1,0:T(8,128)(2,1)S(1)}, u32[]{:S(2)}, u32[]{:S(2)}) async-start(bf16[8,48,384]{2,1,0:T(8,128)(2,1)} %bitcast.8), calls=%async_computation.1 | async-start | bytes 589824 | tf_op jit(solution)/shard_map/all_to_all | solution.py:165
  20.8 14.9 %collective-permute-start.7 = (bf16[384,384]{1,0:T(8,128)(2,1)S(1)}, bf16[384,384]{1,0:T(8,128)(2,1)S(1)}, u32[]{:S(2)}, u32[]{:S(2)}) collective-permute-start(bf16[384,384]{1,0:T(8,128)(2,1)S(1)} %bitcast.25), channel_id=1, source_target_pairs={{0,7},{1,0},{2,1},{3,2},{4,3},{5,4},{6,5},{7,6},{8,15},{9,8},{10,9... | collective-permute-start | bytes 884744 | tf_op jit(solution)/shard_map/ppermute | solution.py:159
  24.0 13.2 %collective-permute-start.1 = (bf16[384,384]{1,0:T(8,128)(2,1)S(1)}, bf16[384,384]{1,0:T(8,128)(2,1)S(1)}, u32[]{:S(2)}, u32[]{:S(2)}) collective-permute-start(bf16[384,384]{1,0:T(8,128)(2,1)S(1)} %collective-permute-done.refs_6_), channel_id=1, source_target_pairs={{0,1},{1,2},{2,3},{3,4},{4,5},{5,6},{6,7},{7,0},{8,9},{9,10},{10,1... | collective-permute-start | bytes 884744 | tf_op jit(solution)/shard_map/ppermute | solution.py:156
  35.6 7.6 %collective-permute-start.8 = (bf16[384,384]{1,0:T(8,128)(2,1)S(1)}, bf16[384,384]{1,0:T(8,128)(2,1)S(1)}, u32[]{:S(2)}, u32[]{:S(2)}) collective-permute-start(bf16[384,384]{1,0:T(8,128)(2,1)S(1)} %collective-permute-done.7.refs_1_), channel_id=1, source_target_pairs={{0,7},{1,0},{2,1},{3,2},{4,3},{5,4},{6,5},{7,6},{8,15},{9,8},{10,9... | collective-permute-start | bytes 884744 | tf_op jit(solution)/shard_map/ppermute | solution.py:159
  37.2 12.2 %collective-permute-start.2 = (bf16[384,384]{1,0:T(8,128)(2,1)S(1)}, bf16[384,384]{1,0:T(8,128)(2,1)S(1)}, u32[]{:S(2)}, u32[]{:S(2)}) collective-permute-start(bf16[384,384]{1,0:T(8,128)(2,1)S(1)} %collective-permute-done.1.refs_5_), channel_id=1, source_target_pairs={{0,1},{1,2},{2,3},{3,4},{4,5},{5,6},{6,7},{7,0},{8,9},{9,10},{10,1... | collective-permute-start | bytes 884744 | tf_op jit(solution)/shard_map/ppermute | solution.py:156
  37.7 11.8 %collective-permute-start.5 = (bf16[384,384]{1,0:T(8,128)(2,1)S(1)}, bf16[384,384]{1,0:T(8,128)(2,1)S(1)}, u32[]{:S(2)}, u32[]{:S(2)}) collective-permute-start(bf16[384,384]{1,0:T(8,128)(2,1)S(1)} %bitcast.20), channel_id=1, source_target_pairs={{0,8},{1,9},{2,10},{3,11},{4,12},{5,13},{6,14},{7,15},{8,16},{9,17... | collective-permute-start | bytes 884744 | tf_op jit(solution)/shard_map/ppermute | solution.py:166
  43.3 11.0 %collective-permute-start.9 = (bf16[384,384]{1,0:T(8,128)(2,1)S(1)}, bf16[384,384]{1,0:T(8,128)(2,1)S(1)}, u32[]{:S(2)}, u32[]{:S(2)}) collective-permute-start(bf16[384,384]{1,0:T(8,128)(2,1)S(1)} %collective-permute-done.8.refs_2_), channel_id=1, source_target_pairs={{0,7},{1,0},{2,1},{3,2},{4,3},{5,4},{6,5},{7,6},{8,15},{9,8},{10,9... | collective-permute-start | bytes 884744 | tf_op jit(solution)/shard_map/ppermute | solution.py:159
  46.7 7.6 %collective-permute-start.4 = (bf16[384,384]{1,0:T(8,128)(2,1)S(1)}, bf16[384,384]{1,0:T(8,128)(2,1)S(1)}, u32[]{:S(2)}, u32[]{:S(2)}) collective-permute-start(bf16[384,384]{1,0:T(8,128)(2,1)S(1)} %bitcast.21), channel_id=1, source_target_pairs={{0,24},{1,25},{2,26},{3,27},{4,28},{5,29},{6,30},{7,31},{8,0},{9,1... | collective-permute-start | bytes 884744 | tf_op jit(solution)/shard_map/ppermute | solution.py:167
  49.4 11.2 %collective-permute-start.3 = (bf16[384,384]{1,0:T(8,128)(2,1)S(1)}, bf16[384,384]{1,0:T(8,128)(2,1)S(1)}, u32[]{:S(2)}, u32[]{:S(2)}) collective-permute-start(bf16[384,384]{1,0:T(8,128)(2,1)S(1)} %collective-permute-done.2.refs_4_), channel_id=1, source_target_pairs={{0,1},{1,2},{2,3},{3,4},{4,5},{5,6},{6,7},{7,0},{8,9},{9,10},{10,1... | collective-permute-start | bytes 884744 | tf_op jit(solution)/shard_map/ppermute | solution.py:156
  49.4 11.2 %collective-permute-start.6 = (bf16[384,384]{1,0:T(8,128)(2,1)S(1)}, bf16[384,384]{1,0:T(8,128)(2,1)S(1)}, u32[]{:S(2)}, u32[]{:S(2)}) collective-permute-start(bf16[384,384]{1,0:T(8,128)(2,1)S(1)} %collective-permute-done.5.refs_9_.m3), channel_id=1, source_target_pairs={{0,8},{1,9},{2,10},{3,11},{4,12},{5,13},{6,14},{7,15},{8,16},{9,17... | collective-permute-start | bytes 884744 | tf_op jit(solution)/shard_map/ppermute | solution.py:168

commit v2 on v1

--- a/solution.py
+++ b/solution.py
@@ -153,11 +153,11 @@
     ints[0] = own_int
     fw = bw = own_int
     for step in range(1, 5):
-        fw = lax.ppermute(fw, "mem", z_perm(1))
-        ints[8 - step] = fw
+        fw = lax.ppermute(fw, "mem", z_perm(-1))
+        ints[step] = fw
         if step < 4:
-            bw = lax.ppermute(bw, "mem", z_perm(-1))
-            ints[step] = bw
+            bw = lax.ppermute(bw, "mem", z_perm(1))
+            ints[8 - step] = bw
 
     doubled = lax.optimization_barrier(2.0 * own_amp.astype(jnp.float32))
     swapped = lax.all_to_all(own_amp, "grp", split_axis=0, concat_axis=0, tiled=True)

time: 102 us -> 102 us (level)
  the two profiles are of different devices: /device:TPU:8 before, /device:TPU:2 now
where the time goes in v2:
time: 102 us
  blocking collectives  33.8 us (33%)
  starting transfers between devices  32.3 us (32%)
  waiting for transfers between devices  17.5 us (17%)
  Pallas kernels  10.3 us (10%)
  other arithmetic  6.96 us (7%)
    all_to_all x1, blocking collectives, local(): lax.all_to_all(part.reshape(NX, NZ * RB, TILE), 'mem', 0, 0, axis_index_g...  17.8 us
    ppermute x3, waiting for transfers between devices, local(): bw = lax.ppermute(bw, 'mem', z_perm(1))  16.4 us
    all_to_all x1, blocking collectives, local(): lax.all_to_all(summed, 'mem', 0, 0, axis_index_groups=Z_GROUPS, tiled=True)  16 us
    ppermute x4, starting transfers between devices, local(): fw = lax.ppermute(fw, 'mem', z_perm(-1))  13.7 us
    all_to_all x1, starting transfers between devices, local(): lax.all_to_all(mixed, 'mem', 0, 0, axis_index_groups=Z_GROUPS, tiled=True)  8.47 us
    pallas_call x1, Pallas kernels, early(): pl.pallas_call(early_kernel, out_shape=(jax.ShapeDtypeStruct((N_MEM, RB,...  6.22 us
    all_to_all x1, starting transfers between devices, local(): lax.all_to_all(own_amp, 'grp', split_axis=0, concat_axis=0, tiled=True)  4.61 us
    sort x1, other arithmetic, task_keys(): keys = lax.sort(key, is_stable=False)  4.26 us
  transfers between devices with their start and end apart: 12, of which 3 were waited for; matrix products, arithmetic and copies ran while one was open for 7% of the time, Pallas kernels for 6%

profile of v2, /device:TPU:2, one launch (start us, length us, event | category | flops | bytes accessed | tf_op | source)
XLA Modules:
  0.0 101.8 jit_solution(16612742469076230930)
XLA Ops:
  0.0 0.0 copy-start
  0.0 0.0 copy-start.1
  0.0 0.0 copy-start.3
  0.0 0.0 copy-start.2
  0.0 4.6 %all-to-all-start = ((bf16[8,48,384]{2,1,0:T(8,128)(2,1)}), bf16[8,48,384]{2,1,0:T(8,128)(2,1)S(1)}, u32[]{:S(2)}, u32[]{:S(2)}) async-start(bf16[8,48,384]{2,1,0:T(8,128)(2,1)} %bitcast.27), calls=%async_computation | async-start | bytes 589824 | tf_op jit(solution)/shard_map/all_to_all | solution.py:163
  4.6 5.9 %collective-permute-start = (bf16[384,384]{1,0:T(8,128)(2,1)}, bf16[384,384]{1,0:T(8,128)(2,1)S(1)}, u32[]{:S(2)}, u32[]{:S(2)}) collective-permute-start(bf16[384,384]{1,0:T(8,128)(2,1)} %bitcast.24), channel_id=1, source_target_pairs={{0,7},{1,0},{2,1},{3,2},{4,3},{5,4},{6,5},{7,6},{8,15},{9,8},{10,9... | collective-permute-start | bytes 884744 | tf_op jit(solution)/shard_map/ppermute | solution.py:156
  10.5 1.0 multiply_bitcast_fusion
  11.5 1.0 all-to-all-done
  12.5 0.8 fusion
  13.3 8.5 %all-to-all-start.1 = ((bf16[8,48,384]{2,1,0:T(8,128)(2,1)}), bf16[8,48,384]{2,1,0:T(8,128)(2,1)S(1)}, u32[]{:S(2)}, u32[]{:S(2)}) async-start(bf16[8,48,384]{2,1,0:T(8,128)(2,1)} %bitcast.8), calls=%async_computation.1 | async-start | bytes 589824 | tf_op jit(solution)/shard_map/all_to_all | solution.py:165
  21.8 0.0 copy-done
  21.8 2.0 %collective-permute-start.7 = (bf16[384,384]{1,0:T(8,128)(2,1)S(1)}, bf16[384,384]{1,0:T(8,128)(2,1)S(1)}, u32[]{:S(2)}, u32[]{:S(2)}) collective-permute-start(bf16[384,384]{1,0:T(8,128)(2,1)S(1)} %bitcast.25), channel_id=1, source_target_pairs={{0,1},{1,2},{2,3},{3,4},{4,5},{5,6},{6,7},{7,0},{8,9},{9,10},{10,1... | collective-permute-start | bytes 884744 | tf_op jit(solution)/shard_map/ppermute | solution.py:159
  23.8 0.0 copy-done.1
  23.8 0.0 collective-permute-done.refs_1_
  23.8 1.4 %collective-permute-start.1 = (bf16[384,384]{1,0:T(8,128)(2,1)S(1)}, bf16[384,384]{1,0:T(8,128)(2,1)S(1)}, u32[]{:S(2)}, u32[]{:S(2)}) collective-permute-start(bf16[384,384]{1,0:T(8,128)(2,1)S(1)} %collective-permute-done.refs_1_), channel_id=1, source_target_pairs={{0,7},{1,0},{2,1},{3,2},{4,3},{5,4},{6,5},{7,6},{8,15},{9,8},{10,9... | collective-permute-start | bytes 884744 | tf_op jit(solution)/shard_map/ppermute | solution.py:156
  25.2 0.0 copy-done.3
  25.2 0.1 iota_compare_fusion.1
  25.3 0.1 lt.64
  25.4 0.0 copy-done.2
  25.4 0.2 select_reduce_fusion
  25.6 12.0 %collective-permute-done.7.refs_6_ = bf16[384,384]{1,0:T(8,128)(2,1)S(1)} collective-permute-done((bf16[384,384]{1,0:T(8,128)(2,1)S(1)}, bf16[384,384]{1,0:T(8,128)(2,1)S(1)}, u32[]{:S(2)}, u32[]{:S(2)}) %collective-permute-start.7) | collective-permute-done | bytes 294944 | tf_op jit(solution)/shard_map/ppermute | solution.py:159
  37.6 0.0 collective-permute-start.8
  37.6 0.0 collective-permute-done.1.refs_2_
  37.6 3.2 %collective-permute-start.2 = (bf16[384,384]{1,0:T(8,128)(2,1)S(1)}, bf16[384,384]{1,0:T(8,128)(2,1)S(1)}, u32[]{:S(2)}, u32[]{:S(2)}) collective-permute-start(bf16[384,384]{1,0:T(8,128)(2,1)S(1)} %collective-permute-done.1.refs_2_), channel_id=1, source_target_pairs={{0,7},{1,0},{2,1},{3,2},{4,3},{5,4},{6,5},{7,6},{8,15},{9,8},{10,9... | collective-permute-start | bytes 884744 | tf_op jit(solution)/shard_map/ppermute | solution.py:156
  40.8 0.0 all-to-all-done.1
  40.8 1.5 %collective-permute-start.5 = (bf16[384,384]{1,0:T(8,128)(2,1)S(1)}, bf16[384,384]{1,0:T(8,128)(2,1)S(1)}, u32[]{:S(2)}, u32[]{:S(2)}) collective-permute-start(bf16[384,384]{1,0:T(8,128)(2,1)S(1)} %bitcast.20), channel_id=1, source_target_pairs={{0,8},{1,9},{2,10},{3,11},{4,12},{5,13},{6,14},{7,15},{8,16},{9,17... | collective-permute-start | bytes 884744 | tf_op jit(solution)/shard_map/ppermute | solution.py:166
  42.3 4.5 %collective-permute-done.8.refs_5_ = bf16[384,384]{1,0:T(8,128)(2,1)S(1)} collective-permute-done((bf16[384,384]{1,0:T(8,128)(2,1)S(1)}, bf16[384,384]{1,0:T(8,128)(2,1)S(1)}, u32[]{:S(2)}, u32[]{:S(2)}) %collective-permute-start.8) | collective-permute-done | bytes 294944 | tf_op jit(solution)/shard_map/ppermute | solution.py:159
  46.8 0.0 collective-permute-start.9
  46.8 0.5 collective-permute-start.4
  47.3 0.0 collective-permute-done.2.refs_3_
  47.3 3.2 %collective-permute-start.3 = (bf16[384,384]{1,0:T(8,128)(2,1)S(1)}, bf16[384,384]{1,0:T(8,128)(2,1)S(1)}, u32[]{:S(2)}, u32[]{:S(2)}) collective-permute-start(bf16[384,384]{1,0:T(8,128)(2,1)S(1)} %collective-permute-done.2.refs_3_), channel_id=1, source_target_pairs={{0,7},{1,0},{2,1},{3,2},{4,3},{5,4},{6,5},{7,6},{8,15},{9,8},{10,9... | collective-permute-start | bytes 884744 | tf_op jit(solution)/shard_map/ppermute | solution.py:156
  50.6 0.0 collective-permute-done.5.refs_9_.m3
  50.6 1.5 %collective-permute-start.6 = (bf16[384,384]{1,0:T(8,128)(2,1)S(1)}, bf16[384,384]{1,0:T(8,128)(2,1)S(1)}, u32[]{:S(2)}, u32[]{:S(2)}) collective-permute-start(bf16[384,384]{1,0:T(8,128)(2,1)S(1)} %collective-permute-done.5.refs_9_.m3), channel_id=1, source_target_pairs={{0,8},{1,9},{2,10},{3,11},{4,12},{5,13},{6,14},{7,15},{8,16},{9,17... | collective-permute-start | bytes 884744 | tf_op jit(solution)/shard_map/ppermute | solution.py:168
  52.1 4.3 %sort.7.keys = s32[2048]{0:T(1024)S(1)} sort(s32[2048]{0:T(1024)S(1)} %add_select_fusion.6), dimensions={0}, to_apply=%region_1.2 | sort | flops 22528 | bytes 16384 | tf_op jit(solution)/shard_map/sort | solution.py:140
  56.4 0.2 convert_reduce_fusion.starts
  56.6 0.0 collective-permute-done.9.refs_4_
  56.6 0.0 collective-permute-done.4.refs_8_.m1
  56.6 6.2 %shard_map.55 = (f32[32,48,384]{2,1,0:T(8,128)S(1)}, bf16[384,2688]{1,0:T(8,128)(2,1)S(1)}) custom-call(s32[2048]{0:T(1024)S(1)} %sort.7.keys, s32[65]{0:T(128)S(1)} %convert_reduce_fusion.starts, bf16[384,384]{1,0:T(8,128)(2,1)S(1)} %bitcast.26, bf16[384,384]{1,0:T(8,128)(2,1)S(1)} %collective-permute-done.refs_1_, ...), custom_call_target="tpu_custom_call" | custom-call | tf_op jit(solution)/shard_map/pallas_call | solution.py:73
  62.9 0.0 collective-permute-done.3.last_tile
  62.9 0.0 collective-permute-done.6.m2
  62.9 4.1 %shard_map.56 = bf16[32,48,384]{2,1,0:T(8,128)(2,1)S(1)} custom-call(s32[2048]{0:T(1024)S(1)} %sort.7.keys, s32[65]{0:T(128)S(1)} %convert_reduce_fusion.starts, bf16[384,384]{1,0:T(8,128)(2,1)S(1)} %collective-permute-done.3.last_tile, bf16[384,384]{1,0:T(8,128)(2,1)S(1)} %bitcast.23, bf16[384,384]{1,0:T(8,128)(2,1)S(1)} %collective-permute-done.4.refs_8_.m1, ...), custom_call_target="tpu_custom_call" | custom-call | tf_op jit(solution)/shard_map/pallas_call | solution.py:114
  67.0 17.8 %all_to_all.34 = bf16[4,384,384]{2,1,0:T(8,128)(2,1)S(1)} all-to-all(bf16[4,384,384]{2,1,0:T(8,128)(2,1)S(1)} %bitcast.19), channel_id=1, replica_groups={{0,8,16,24},{1,9,17,25},{2,10,18,26},{3,11,19,27},{4,12,20,28},{5,13,21..., dimensions={0} | all-to-all | bytes 2359296 | tf_op jit(solution)/shard_map/all_to_all | solution.py:173
  84.8 0.3 reduce_sum.32
  85.1 16.0 %all_to_all.35 = bf16[8,48,384]{2,1,0:T(8,128)(2,1)S(1)} all-to-all(bf16[8,48,384]{2,1,0:T(8,128)(2,1)S(1)} %bitcast.29), channel_id=1, replica_groups={{0,1,2,3,4,5,6,7},{8,9,10,11,12,13,14,15},{16,17,18,19,20,21,22,23},{24..., dimensions={0} | all-to-all | bytes 589824 | tf_op jit(solution)/shard_map/all_to_all | solution.py:177
  101.1 0.7 copy.12
  (4 shorter events, 0.1 us)
Async XLA Ops:
  0.0 21.8 %copy-start = (bf16[1,1,384,384]{3,2,1,0:T(8,128)(2,1)S(1)}, bf16[1,1,384,384]{3,2,1,0:T(8,128)(2,1)}, u32[]{:S(2)}) copy-start(bf16[1,1,384,384]{3,2,1,0:T(8,128)(2,1)} %param.6) | copy-start | bytes 884740
  0.0 23.8 %copy-start.1 = (s32[1,2048,3]{1,0,2:T(1,128)S(1)}, s32[1,2048,3]{1,0,2:T(1,128)}, u32[]{:S(2)}) copy-start(s32[1,2048,3]{1,0,2:T(1,128)} %param.7) | copy-start | bytes 73732
  0.0 25.2 %copy-start.3 = (s32[1,32]{1,0:T(1,128)S(1)}, s32[1,32]{1,0:T(1,128)}, u32[]{:S(2)}) copy-start(s32[1,32]{1,0:T(1,128)} %param.8) | copy-start | bytes 388
  0.0 25.4 %copy-start.2 = (s32[32]{0:T(128)S(1)}, s32[32]{0:T(128)}, u32[]{:S(2)}) copy-start(s32[32]{0:T(128)} %param.9) | copy-start | bytes 388
  0.0 12.5 %all-to-all-start = ((bf16[8,48,384]{2,1,0:T(8,128)(2,1)}), bf16[8,48,384]{2,1,0:T(8,128)(2,1)S(1)}, u32[]{:S(2)}, u32[]{:S(2)}) async-start(bf16[8,48,384]{2,1,0:T(8,128)(2,1)} %bitcast.27), calls=%async_computation | async-start | bytes 589824 | tf_op jit(solution)/shard_map/all_to_all | solution.py:163
  4.6 19.2 %collective-permute-start = (bf16[384,384]{1,0:T(8,128)(2,1)}, bf16[384,384]{1,0:T(8,128)(2,1)S(1)}, u32[]{:S(2)}, u32[]{:S(2)}) collective-permute-start(bf16[384,384]{1,0:T(8,128)(2,1)} %bitcast.24), channel_id=1, source_target_pairs={{0,7},{1,0},{2,1},{3,2},{4,3},{5,4},{6,5},{7,6},{8,15},{9,8},{10,9... | collective-permute-start | bytes 884744 | tf_op jit(solution)/shard_map/ppermute | solution.py:156
  13.3 27.5 %all-to-all-start.1 = ((bf16[8,48,384]{2,1,0:T(8,128)(2,1)}), bf16[8,48,384]{2,1,0:T(8,128)(2,1)S(1)}, u32[]{:S(2)}, u32[]{:S(2)}) async-start(bf16[8,48,384]{2,1,0:T(8,128)(2,1)} %bitcast.8), calls=%async_computation.1 | async-start | bytes 589824 | tf_op jit(solution)/shard_map/all_to_all | solution.py:165
  21.8 15.8 %collective-permute-start.7 = (bf16[384,384]{1,0:T(8,128)(2,1)S(1)}, bf16[384,384]{1,0:T(8,128)(2,1)S(1)}, u32[]{:S(2)}, u32[]{:S(2)}) collective-permute-start(bf16[384,384]{1,0:T(8,128)(2,1)S(1)} %bitcast.25), channel_id=1, source_target_pairs={{0,1},{1,2},{2,3},{3,4},{4,5},{5,6},{6,7},{7,0},{8,9},{9,10},{10,1... | collective-permute-start | bytes 884744 | tf_op jit(solution)/shard_map/ppermute | solution.py:159
  23.8 13.7 %collective-permute-start.1 = (bf16[384,384]{1,0:T(8,128)(2,1)S(1)}, bf16[384,384]{1,0:T(8,128)(2,1)S(1)}, u32[]{:S(2)}, u32[]{:S(2)}) collective-permute-start(bf16[384,384]{1,0:T(8,128)(2,1)S(1)} %collective-permute-done.refs_1_), channel_id=1, source_target_pairs={{0,7},{1,0},{2,1},{3,2},{4,3},{5,4},{6,5},{7,6},{8,15},{9,8},{10,9... | collective-permute-start | bytes 884744 | tf_op jit(solution)/shard_map/ppermute | solution.py:156
  37.6 9.2 %collective-permute-start.8 = (bf16[384,384]{1,0:T(8,128)(2,1)S(1)}, bf16[384,384]{1,0:T(8,128)(2,1)S(1)}, u32[]{:S(2)}, u32[]{:S(2)}) collective-permute-start(bf16[384,384]{1,0:T(8,128)(2,1)S(1)} %collective-permute-done.7.refs_6_), channel_id=1, source_target_pairs={{0,1},{1,2},{2,3},{3,4},{4,5},{5,6},{6,7},{7,0},{8,9},{9,10},{10,1... | collective-permute-start | bytes 884744 | tf_op jit(solution)/shard_map/ppermute | solution.py:159
  37.6 9.7 %collective-permute-start.2 = (bf16[384,384]{1,0:T(8,128)(2,1)S(1)}, bf16[384,384]{1,0:T(8,128)(2,1)S(1)}, u32[]{:S(2)}, u32[]{:S(2)}) collective-permute-start(bf16[384,384]{1,0:T(8,128)(2,1)S(1)} %collective-permute-done.1.refs_2_), channel_id=1, source_target_pairs={{0,7},{1,0},{2,1},{3,2},{4,3},{5,4},{6,5},{7,6},{8,15},{9,8},{10,9... | collective-permute-start | bytes 884744 | tf_op jit(solution)/shard_map/ppermute | solution.py:156
  40.8 9.7 %collective-permute-start.5 = (bf16[384,384]{1,0:T(8,128)(2,1)S(1)}, bf16[384,384]{1,0:T(8,128)(2,1)S(1)}, u32[]{:S(2)}, u32[]{:S(2)}) collective-permute-start(bf16[384,384]{1,0:T(8,128)(2,1)S(1)} %bitcast.20), channel_id=1, source_target_pairs={{0,8},{1,9},{2,10},{3,11},{4,12},{5,13},{6,14},{7,15},{8,16},{9,17... | collective-permute-start | bytes 884744 | tf_op jit(solution)/shard_map/ppermute | solution.py:166
  46.8 9.8 %collective-permute-start.9 = (bf16[384,384]{1,0:T(8,128)(2,1)S(1)}, bf16[384,384]{1,0:T(8,128)(2,1)S(1)}, u32[]{:S(2)}, u32[]{:S(2)}) collective-permute-start(bf16[384,384]{1,0:T(8,128)(2,1)S(1)} %collective-permute-done.8.refs_5_), channel_id=1, source_target_pairs={{0,1},{1,2},{2,3},{3,4},{4,5},{5,6},{6,7},{7,0},{8,9},{9,10},{10,1... | collective-permute-start | bytes 884744 | tf_op jit(solution)/shard_map/ppermute | solution.py:159
  46.8 9.8 %collective-permute-start.4 = (bf16[384,384]{1,0:T(8,128)(2,1)S(1)}, bf16[384,384]{1,0:T(8,128)(2,1)S(1)}, u32[]{:S(2)}, u32[]{:S(2)}) collective-permute-start(bf16[384,384]{1,0:T(8,128)(2,1)S(1)} %bitcast.21), channel_id=1, source_target_pairs={{0,24},{1,25},{2,26},{3,27},{4,28},{5,29},{6,30},{7,31},{8,0},{9,1... | collective-permute-start | bytes 884744 | tf_op jit(solution)/shard_map/ppermute | solution.py:167
  47.3 15.5 %collective-permute-start.3 = (bf16[384,384]{1,0:T(8,128)(2,1)S(1)}, bf16[384,384]{1,0:T(8,128)(2,1)S(1)}, u32[]{:S(2)}, u32[]{:S(2)}) collective-permute-start(bf16[384,384]{1,0:T(8,128)(2,1)S(1)} %collective-permute-done.2.refs_3_), channel_id=1, source_target_pairs={{0,7},{1,0},{2,1},{3,2},{4,3},{5,4},{6,5},{7,6},{8,15},{9,8},{10,9... | collective-permute-start | bytes 884744 | tf_op jit(solution)/shard_map/ppermute | solution.py:156
  50.6 12.3 %collective-permute-start.6 = (bf16[384,384]{1,0:T(8,128)(2,1)S(1)}, bf16[384,384]{1,0:T(8,128)(2,1)S(1)}, u32[]{:S(2)}, u32[]{:S(2)}) collective-permute-start(bf16[384,384]{1,0:T(8,128)(2,1)S(1)} %collective-permute-done.5.refs_9_.m3), channel_id=1, source_target_pairs={{0,8},{1,9},{2,10},{3,11},{4,12},{5,13},{6,14},{7,15},{8,16},{9,17... | collective-permute-start | bytes 884744 | tf_op jit(solution)/shard_map/ppermute | solution.py:168
